TPU v7x, 128 devices: a whole 4x4x4 slice. The times are simulated.
128 devices in a mesh: lag: 16 (over z_lo, x, core), row: 8 (over y, z_hi).
Axes of the slice: x: 4, y: 4, z: 4 (z_hi: 2, z_lo: 2; z = z_hi * 2 + z_lo), core: 2. Of those that a mesh axis runs over, the one named last changes fastest.
Arguments:
- lag_matrix: bfloat16 [16, 8192, 8192], P('lag', 'row'), may hold values from -0.015625 to 0.015625
- past_current: bfloat16 [16, 256, 8192], P('lag', None, 'row'), may hold values from -6 to 6
- excitation: float32 [2, 256, 8192], P(None, None, 'row'), may hold values from -6 to 6
- block_inverse: float32 [64, 128, 128], P('row'), may hold values from -2 to 3
Outputs:
- currents: bfloat16 [2, 256, 8192], P(None, 'lag', 'row')
All inputs are finite; a program needn't handle non-finite values.
Results may differ from a plain program's by a relative error of at most 0.002.
Values may be sent and summed in bfloat16 or wider, within the bound.
A program may use at most 64 MiB of HBM per device.

v0:
```python
import jax
import jax.numpy as jnp
from jax import lax
from jax.sharding import PartitionSpec as P

STEPS = 2


def in_blocks(x, dim, peers):
    before, after = (x.shape[:dim], x.shape[dim + 1 :])
    return jnp.moveaxis(x.reshape(*before, peers, -1, *after), dim, 0)


def summed_on_arrival(x, axis, dim):
    tiles = in_blocks(x, dim, lax.axis_size(axis))
    arrived = lax.all_to_all(tiles, axis, split_axis=0, concat_axis=0, tiled=True)
    return arrived.sum(axis=0)


def in_order(tiles, dim):
    tiles = jnp.moveaxis(tiles, 0, dim)
    lengths = tiles.shape
    return tiles.reshape(*lengths[:dim], lengths[dim] * lengths[dim + 1], *lengths[dim + 2 :])


def from_everyone(x, axis):
    peers = lax.axis_size(axis)
    return lax.all_to_all(jnp.broadcast_to(x[None], (peers, *x.shape)), axis, 0, 0, tiled=True)


def gather_directly(x, axis, dim):
    return in_order(from_everyone(x, axis), dim)


def from_behind(x, axis, by):
    peers = lax.axis_size(axis)
    pairs = [(i, i + by) for i in range(peers) if 0 <= i + by < peers]
    return lax.ppermute(x, axis, pairs)


def solve_blocks(source, block_inverse):
    count = source.shape[0]
    pieces = source.reshape(count, block_inverse.shape[0], block_inverse.shape[1])
    result = jnp.einsum("bij,rbj->rbi", block_inverse, pieces, precision=lax.Precision.HIGHEST)
    return result.reshape(count, source.shape[1]).astype(jnp.bfloat16)


def advance(older, newest, leading):
    incoming_rest = jnp.concatenate([older, leading[:-1]], axis=0)
    first = lax.axis_index("lag") == 0
    head = jnp.where(first, newest[None], incoming_rest)
    return jnp.concatenate([head, incoming_rest[1:]], axis=0)


def per_device(lag_matrix, past_current, excitation, block_inverse):
    lag_count = lax.axis_size("lag")
    excite_all = past_current.shape[1]
    share = excite_all // lag_count
    offset = lax.axis_index("lag") * share
    current_loc = past_current
    results = []
    for step in range(STEPS):
        partial_value = jnp.einsum(
            "lrc,lkc->rk",
            lax.all_gather(current_loc, "row", axis=2, tiled=True),
            lag_matrix,
            preferred_element_type=jnp.float32,
        )
        history = summed_on_arrival(partial_value, "lag", 0)
        mine = lax.dynamic_slice_in_dim(excitation[step], offset, share, 0)
        newest_part = solve_blocks(mine - history, block_inverse)
        results.append(newest_part)
        if step + 1 < STEPS:
            newest = gather_directly(newest_part, "lag", 0)
        if step + 1 < STEPS:
            older = from_behind(current_loc, "lag", 1)
            current_loc = advance(older, newest, current_loc)
    return jnp.stack(results)


def solution(mesh):
    in_specs = (
        P("lag", "row", None),
        P("lag", None, "row"),
        P(None, None, "row"),
        P("row", None, None),
    )
    out_specs = P(None, "lag", "row")
    return jax.shard_map(
        per_device, mesh=mesh, in_specs=in_specs, out_specs=out_specs, check_vma=False
    )
```

profile of v0, /device:TPU:1, one launch (start us, length us, event | category | flops | bytes accessed | tf_op | source)
XLA Modules:
  0.0 246.1 jit_solution(4965949983607384674)
XLA Ops:
  6.5 0.0 copy-start
  6.5 0.0 all-gather.3.cloned.1.call-start
  6.5 0.7 all-gather.3.cloned.1.call-update
  7.3 76.9 %all-gather.3.cloned.1.call-done = bf16[1,256,8192]{2,1,0:T(8,128)(2,1)} async-done(((bf16[1,256,1024]{2,1,0:T(8,128)(2,1)}), bf16[1,256,8192]{2,1,0:T(8,128)(2,1)}) %all-gather.3.cloned.1.call-update) | async-done | bytes 4194320 | tf_op jit(solution)/shard_map/all_gather | solution.py:65
  84.2 0.0 copy-start.1
  84.2 12.6 %fusion.2 = f32[16,16,1024]{2,1,0:T(8,128)} fusion(bf16[16,16,8192]{2,1,0:T(8,128)(2,1)} %bitcast.44, bf16[1,1024,8192]{2,1,0:T(8,128)(2,1)} %param.4), kind=kOutput, calls=%fused_computation.2 | convolution fusion | flops 4294967296 | bytes 22020096 | tf_op jit(solution)/shard_map/lrc,lkc->rk/dot_general | solution.py:63
  96.7 5.4 %all-to-all-start = ((f32[16,16,1024]{2,1,0:T(8,128)}), f32[16,16,1024]{2,1,0:T(8,128)S(1)}, u32[]{:S(2)}, u32[]{:S(2)}) async-start(f32[16,16,1024]{2,1,0:T(8,128)} %fusion.2), calls=%async_computation | async-start | bytes 2097152 | tf_op jit(solution)/shard_map/all_to_all | solution.py:16
  102.2 0.0 copy-done.1
  102.2 3.5 %collective-permute-start = (bf16[1,256,1024]{2,1,0:T(8,128)(2,1)S(1)}, bf16[1,256,1024]{2,1,0:T(8,128)(2,1)}, u32[]{:S(2)}, u32[]{:S(2)}) collective-permute-start(bf16[1,256,1024]{2,1,0:T(8,128)(2,1)S(1)} %copy-done.1), channel_id=1, source_target_pairs={{0,8},{8,16},{16,24},{24,32},{32,40},{40,48},{48,56},{56,64},{64,7... | collective-permute-start | bytes 1572872 | tf_op jit(solution)/shard_map/ppermute | solution.py:38
  105.7 1.7 fusion.7
  107.5 10.6 %all-to-all-done = f32[16,16,1024]{2,1,0:T(8,128)S(1)} async-done(((f32[16,16,1024]{2,1,0:T(8,128)}), f32[16,16,1024]{2,1,0:T(8,128)S(1)}, u32[]{:S(2)}, u32[]{:S(2)}) %all-to-all-start) | async-done | bytes 1048608 | tf_op jit(solution)/shard_map/all_to_all | solution.py:16
  118.0 0.1 reduce_sum.22
  118.1 0.0 copy-done
  118.1 0.9 convolution_convert_fusion.1
  119.0 0.9 broadcast_in_dim.2
  119.9 4.1 %all-to-all-start.1 = ((bf16[16,16,1024]{2,1,0:T(8,128)(2,1)}), bf16[16,16,1024]{2,1,0:T(8,128)(2,1)S(1)}, u32[]{:S(2)}, u32[]{:S(2)}) async-start(bf16[16,16,1024]{2,1,0:T(8,128)(2,1)} %broadcast_in_dim.2), calls=%async_computation.1 | async-start | bytes 1048576 | tf_op jit(solution)/shard_map/all_to_all | solution.py:28
  124.0 0.0 all-gather.5.cloned.1.call-start
  124.0 0.0 collective-permute-done
  124.0 9.9 %all-to-all-done.1 = bf16[16,16,1024]{2,1,0:T(8,128)(2,1)S(1)} async-done(((bf16[16,16,1024]{2,1,0:T(8,128)(2,1)}), bf16[16,16,1024]{2,1,0:T(8,128)(2,1)S(1)}, u32[]{:S(2)}, u32[]{:S(2)}) %all-to-all-start.1) | async-done | bytes 524320 | tf_op jit(solution)/shard_map/all_to_all | solution.py:28
  134.0 1.9 bitcast_select_fusion
  135.9 0.0 all-gather.5.cloned.1.call-update
  135.9 67.8 %all-gather.5.cloned.1.call-done = bf16[1,256,8192]{2,1,0:T(8,128)(2,1)} async-done(((bf16[1,256,1024]{2,1,0:T(8,128)(2,1)}), bf16[1,256,8192]{2,1,0:T(8,128)(2,1)}) %all-gather.5.cloned.1.call-update) | async-done | bytes 4194320 | tf_op jit(solution)/shard_map/all_gather | solution.py:65
  203.7 12.5 %fusion = f32[16,16,1024]{2,1,0:T(8,128)} fusion(bf16[16,16,8192]{2,1,0:T(8,128)(2,1)} %bitcast.43, bf16[1,1024,8192]{2,1,0:T(8,128)(2,1)} %param.4), kind=kOutput, calls=%fused_computation | convolution fusion | flops 4294967296 | bytes 22020096 | tf_op jit(solution)/shard_map/lrc,lkc->rk/dot_general | solution.py:63
  216.2 5.4 %all-to-all-start.2 = ((f32[16,16,1024]{2,1,0:T(8,128)}), f32[16,16,1024]{2,1,0:T(8,128)S(1)}, u32[]{:S(2)}, u32[]{:S(2)}) async-start(f32[16,16,1024]{2,1,0:T(8,128)} %fusion), calls=%async_computation.2 | async-start | bytes 2097152 | tf_op jit(solution)/shard_map/all_to_all | solution.py:16
  221.7 15.8 %all-to-all-done.2 = f32[16,16,1024]{2,1,0:T(8,128)S(1)} async-done(((f32[16,16,1024]{2,1,0:T(8,128)}), f32[16,16,1024]{2,1,0:T(8,128)S(1)}, u32[]{:S(2)}, u32[]{:S(2)}) %all-to-all-start.2) | async-done | bytes 1048608 | tf_op jit(solution)/shard_map/all_to_all | solution.py:16
  237.5 0.1 reduce_sum.24
  237.6 0.9 fusion.4
  238.6 0.6 pad_maximum_fusion
  (13 shorter events, 0.2 us)
Async XLA Ops:
  6.5 111.6 %copy-start = (f32[8,128,128]{2,1,0:T(8,128)S(1)}, f32[8,128,128]{2,1,0:T(8,128)}, u32[]{:S(2)}) copy-start(f32[8,128,128]{2,1,0:T(8,128)} %param.7) | copy-start | bytes 1572868
  6.5 77.6 %all-gather.3.cloned.1.call-start = ((), (), s32[]{:S(2)}) async-start(), calls=%async_computation.3 | async-start | bytes 4718592 | tf_op jit(solution)/shard_map/all_gather | solution.py:65
  84.2 18.0 %copy-start.1 = (bf16[1,256,1024]{2,1,0:T(8,128)(2,1)S(1)}, bf16[1,256,1024]{2,1,0:T(8,128)(2,1)}, u32[]{:S(2)}) copy-start(bf16[1,256,1024]{2,1,0:T(8,128)(2,1)} %param.5) | copy-start | bytes 1572868
  96.7 21.3 %all-to-all-start = ((f32[16,16,1024]{2,1,0:T(8,128)}), f32[16,16,1024]{2,1,0:T(8,128)S(1)}, u32[]{:S(2)}, u32[]{:S(2)}) async-start(f32[16,16,1024]{2,1,0:T(8,128)} %fusion.2), calls=%async_computation | async-start | bytes 2097152 | tf_op jit(solution)/shard_map/all_to_all | solution.py:16
  102.2 21.9 %collective-permute-start = (bf16[1,256,1024]{2,1,0:T(8,128)(2,1)S(1)}, bf16[1,256,1024]{2,1,0:T(8,128)(2,1)}, u32[]{:S(2)}, u32[]{:S(2)}) collective-permute-start(bf16[1,256,1024]{2,1,0:T(8,128)(2,1)S(1)} %copy-done.1), channel_id=1, source_target_pairs={{0,8},{8,16},{16,24},{24,32},{32,40},{40,48},{48,56},{56,64},{64,7... | collective-permute-start | bytes 1572872 | tf_op jit(solution)/shard_map/ppermute | solution.py:38
  119.9 14.1 %all-to-all-start.1 = ((bf16[16,16,1024]{2,1,0:T(8,128)(2,1)}), bf16[16,16,1024]{2,1,0:T(8,128)(2,1)S(1)}, u32[]{:S(2)}, u32[]{:S(2)}) async-start(bf16[16,16,1024]{2,1,0:T(8,128)(2,1)} %broadcast_in_dim.2), calls=%async_computation.1 | async-start | bytes 1048576 | tf_op jit(solution)/shard_map/all_to_all | solution.py:28
  124.0 79.7 %all-gather.5.cloned.1.call-start = ((), (), s32[]{:S(2)}) async-start(), calls=%async_computation.4 | async-start | bytes 4718592 | tf_op jit(solution)/shard_map/all_gather | solution.py:65
  216.2 21.3 %all-to-all-start.2 = ((f32[16,16,1024]{2,1,0:T(8,128)}), f32[16,16,1024]{2,1,0:T(8,128)S(1)}, u32[]{:S(2)}, u32[]{:S(2)}) async-start(f32[16,16,1024]{2,1,0:T(8,128)} %fusion), calls=%async_computation.2 | async-start | bytes 2097152 | tf_op jit(solution)/shard_map/all_to_all | solution.py:16
Sparse Core Ops, SparseCore 0:
  9.7 74.3 all-gather.2
  136.0 67.6 all-gather.4
where the time goes:
time: 247 us; the launch traced here: 246 us
  waiting for transfers between devices  182 us (74%)
  matrix products  26.9 us (11%)
  starting transfers between devices  18.5 us (7%)
  between operations  13.5 us (5%)
  local copies, waits for them, and re-layouts  2.71 us (1%)
  other arithmetic  2.68 us (1%)
    all_gather x2, waiting for transfers between devices, per_device(): lax.all_gather(current_loc, 'row', axis=2, tiled=True)  145 us
    all_to_all x2, waiting for transfers between devices, summed_on_arrival(): lax.all_to_all(tiles, axis, split_axis=0, concat_axis=0, tiled=True)  26.3 us
    dot_general x2, matrix products, per_device(): jnp.einsum('lrc,lkc->rk', lax.all_gather(current_loc, 'row', axis=2, tile...  25.1 us
    all_to_all x2, starting transfers between devices, summed_on_arrival(): lax.all_to_all(tiles, axis, split_axis=0, concat_axis=0, tiled=True)  10.9 us
    all_to_all x1, waiting for transfers between devices, from_everyone(): lax.all_to_all(jnp.broadcast_to(x[None], (peers, *x.shape)), axis, 0, 0,...  9.92 us
  transfers between devices with their start and end apart: 6, of which 5 were waited for; matrix products, arithmetic and copies ran while one was open for 1% of the time, Pallas kernels for 0%

commit v1 on v0

--- a/solution.py
+++ b/solution.py
@@ -62,7 +62,9 @@
     for step in range(STEPS):
         partial_value = jnp.einsum(
             "lrc,lkc->rk",
-            lax.all_gather(current_loc, "row", axis=2, tiled=True),
+            jnp.concatenate(
+                lax.all_to_all(jnp.stack([current_loc] * lax.axis_size("row")), "row", 0, 0), axis=2
+            ),
             lag_matrix,
             preferred_element_type=jnp.float32,
         )

time: 247 us -> 225 us (0.911)
  waiting for transfers between devices: 182 us -> 36.4 us
  blocking collectives: 0 us -> 111 us
  local copies, waits for them, and re-layouts: 2.71 us -> 28.2 us
  between operations: 13.5 us -> 0.16 us
    all_gather x2 -> x0, waiting for transfers between devices: 145 us -> none  [per_device(): lax.all_gather(current_loc, 'row', axis=2, tiled=True)]
    all_to_all x0 -> x2, blocking collectives: none -> 111 us  [per_device(): lax.all_to_all(jnp.stack([current_loc] * lax.axis_size('row')), 'row', 0, 0)]
    dot_general x0 -> x2, local copies, waits for them, and re-layouts: none -> 14.8 us  [per_device(): jnp.einsum('lrc,lkc->rk', jnp.concatenate(lax.all_to_all(jnp.stack([curre...]
    reshape x0 -> x2, local copies, waits for them, and re-layouts: none -> 8.58 us  [per_device(): jnp.concatenate(lax.all_to_all(jnp.stack([current_loc] * lax.axis_size('r...]
  transfers between devices with their start and end apart: 6 -> 4, of which waited for: 5 -> 3; matrix products, arithmetic and copies ran while one was open for 1% -> 2% of each run, Pallas kernels for 0% -> 0%
where the time goes in v1:
time: 225 us; the launch traced here: 224 us
  blocking collectives  111 us (49%)
  waiting for transfers between devices  36.4 us (16%)
  local copies, waits for them, and re-layouts  28.2 us (13%)
  matrix products  27 us (12%)
  starting transfers between devices  19.5 us (9%)
    all_to_all x2, blocking collectives, per_device(): lax.all_to_all(jnp.stack([current_loc] * lax.axis_size('row')), 'row', 0, 0)  111 us
    all_to_all x2, waiting for transfers between devices, summed_on_arrival(): lax.all_to_all(tiles, axis, split_axis=0, concat_axis=0, tiled=True)  26.4 us
    dot_general x2, matrix products, per_device(): jnp.einsum('lrc,lkc->rk', jnp.concatenate(lax.all_to_all(jnp.stack([curre...  25.1 us
    dot_general x2, local copies, waits for them, and re-layouts, per_device(): jnp.einsum('lrc,lkc->rk', jnp.concatenate(lax.all_to_all(jnp.stack([curre...  14.8 us
    all_to_all x2, starting transfers between devices, summed_on_arrival(): lax.all_to_all(tiles, axis, split_axis=0, concat_axis=0, tiled=True)  11.9 us
    all_to_all x1, waiting for transfers between devices, from_everyone(): lax.all_to_all(jnp.broadcast_to(x[None], (peers, *x.shape)), axis, 0, 0,...  9.98 us
    reshape x2, local copies, waits for them, and re-layouts, per_device(): jnp.concatenate(lax.all_to_all(jnp.stack([current_loc] * lax.axis_size('r...  8.58 us
  transfers between devices with their start and end apart: 4, of which 3 were waited for; matrix products, arithmetic and copies ran while one was open for 2% of the time, Pallas kernels for 0%

profile of v1, /device:TPU:1, one launch (start us, length us, event | category | flops | bytes accessed | tf_op | source)
XLA Modules:
  0.0 224.4 jit_solution(11821504928805476751)
XLA Ops:
  0.0 0.0 copy-start
  0.0 1.6 stack.6
  1.6 57.3 %all_to_all.25 = bf16[8,1,256,1024]{3,2,1,0:T(8,128)(2,1)S(1)} all-to-all(bf16[8,1,256,1024]{3,2,1,0:T(8,128)(2,1)S(1)} %stack.6), channel_id=1, replica_groups=mesh['lag'=16,'row'=8] {'row'}, dimensions={0} | all-to-all | bytes 8388608 | tf_op jit(solution)/shard_map/all_to_all | solution.py:66
  59.0 4.3 %copy.10 = bf16[1,256,8,1024]{3,2,1,0:T(8,128)(2,1)} copy(bf16[1,256,8,1024]{3,1,0,2:T(8,128)(2,1)S(1)} %bitcast.48) | data formatting | bytes 8388608 | tf_op jit(solution)/shard_map/reshape | solution.py:65
  63.3 7.4 %dot_general.16 = bf16[16,16,8192]{2,1,0:T(8,128)(2,1)} reshape(bf16[1,256,8,1024]{3,2,1,0:T(8,128)(2,1)} %copy.10) | data formatting | bytes 8388608 | tf_op jit(solution)/shard_map/lrc,lkc->rk/dot_general | solution.py:63
  70.7 0.0 copy-start.1
  70.7 12.6 %fusion.2 = f32[16,16,1024]{2,1,0:T(8,128)} fusion(bf16[16,16,8192]{2,1,0:T(8,128)(2,1)} %dot_general.16, bf16[1,1024,8192]{2,1,0:T(8,128)(2,1)} %param.4), kind=kOutput, calls=%fused_computation.2 | convolution fusion | flops 4294967296 | bytes 22020096 | tf_op jit(solution)/shard_map/lrc,lkc->rk/dot_general | solution.py:63
  83.2 7.3 %all-to-all-start.1 = ((f32[16,16,1024]{2,1,0:T(8,128)}), f32[16,16,1024]{2,1,0:T(8,128)S(1)}, u32[]{:S(2)}, u32[]{:S(2)}) async-start(f32[16,16,1024]{2,1,0:T(8,128)} %fusion.2), calls=%async_computation.1 | async-start | bytes 2097152 | tf_op jit(solution)/shard_map/all_to_all | solution.py:16
  90.5 0.0 copy-done.1
  90.5 3.5 %collective-permute-start = (bf16[1,256,1024]{2,1,0:T(8,128)(2,1)S(1)}, bf16[1,256,1024]{2,1,0:T(8,128)(2,1)}, u32[]{:S(2)}, u32[]{:S(2)}) collective-permute-start(bf16[1,256,1024]{2,1,0:T(8,128)(2,1)S(1)} %copy-done.1), channel_id=1, source_target_pairs={{0,8},{8,16},{16,24},{24,32},{32,40},{40,48},{48,56},{56,64},{64,7... | collective-permute-start | bytes 1572872 | tf_op jit(solution)/shard_map/ppermute | solution.py:38
  94.1 1.7 fusion.8
  95.8 10.6 %all-to-all-done.1 = f32[16,16,1024]{2,1,0:T(8,128)S(1)} async-done(((f32[16,16,1024]{2,1,0:T(8,128)}), f32[16,16,1024]{2,1,0:T(8,128)S(1)}, u32[]{:S(2)}, u32[]{:S(2)}) %all-to-all-start.1) | async-done | bytes 1048608 | tf_op jit(solution)/shard_map/all_to_all | solution.py:16
  106.4 0.1 reduce_sum.22
  106.5 0.0 copy-done
  106.5 0.9 convolution_convert_fusion.1
  107.4 0.9 broadcast_in_dim.2
  108.3 4.1 %all-to-all-start.2 = ((bf16[16,16,1024]{2,1,0:T(8,128)(2,1)}), bf16[16,16,1024]{2,1,0:T(8,128)(2,1)S(1)}, u32[]{:S(2)}, u32[]{:S(2)}) async-start(bf16[16,16,1024]{2,1,0:T(8,128)(2,1)} %broadcast_in_dim.2), calls=%async_computation.2 | async-start | bytes 1048576 | tf_op jit(solution)/shard_map/all_to_all | solution.py:28
  112.4 0.0 collective-permute-done
  112.4 10.0 %all-to-all-done.2 = bf16[16,16,1024]{2,1,0:T(8,128)(2,1)S(1)} async-done(((bf16[16,16,1024]{2,1,0:T(8,128)(2,1)}), bf16[16,16,1024]{2,1,0:T(8,128)(2,1)S(1)}, u32[]{:S(2)}, u32[]{:S(2)}) %all-to-all-start.2) | async-done | bytes 524320 | tf_op jit(solution)/shard_map/all_to_all | solution.py:28
  122.3 1.1 fusion.5
  123.4 0.5 stack.7
  124.0 54.0 %all_to_all.26 = bf16[8,1,256,1024]{3,2,1,0:T(8,128)(2,1)S(1)} all-to-all(bf16[8,1,256,1024]{3,2,1,0:T(8,128)(2,1)S(1)} %stack.7), channel_id=1, replica_groups=mesh['lag'=16,'row'=8] {'row'}, dimensions={0} | all-to-all | bytes 8388608 | tf_op jit(solution)/shard_map/all_to_all | solution.py:66
  178.0 4.3 %copy.14 = bf16[1,256,8,1024]{3,2,1,0:T(8,128)(2,1)} copy(bf16[1,256,8,1024]{3,1,0,2:T(8,128)(2,1)S(1)} %bitcast.49) | data formatting | bytes 8388608 | tf_op jit(solution)/shard_map/reshape | solution.py:65
  182.3 7.4 %dot_general.19 = bf16[16,16,8192]{2,1,0:T(8,128)(2,1)} reshape(bf16[1,256,8,1024]{3,2,1,0:T(8,128)(2,1)} %copy.14) | data formatting | bytes 8388608 | tf_op jit(solution)/shard_map/lrc,lkc->rk/dot_general | solution.py:63
  189.6 12.5 %fusion = f32[16,16,1024]{2,1,0:T(8,128)} fusion(bf16[16,16,8192]{2,1,0:T(8,128)(2,1)} %dot_general.19, bf16[1,1024,8192]{2,1,0:T(8,128)(2,1)} %param.4), kind=kOutput, calls=%fused_computation | convolution fusion | flops 4294967296 | bytes 22020096 | tf_op jit(solution)/shard_map/lrc,lkc->rk/dot_general | solution.py:63
  202.2 4.6 %all-to-all-start.4 = ((f32[16,16,1024]{2,1,0:T(8,128)}), f32[16,16,1024]{2,1,0:T(8,128)S(1)}, u32[]{:S(2)}, u32[]{:S(2)}) async-start(f32[16,16,1024]{2,1,0:T(8,128)} %fusion), calls=%async_computation.4 | async-start | bytes 2097152 | tf_op jit(solution)/shard_map/all_to_all | solution.py:16
  206.8 15.9 %all-to-all-done.4 = f32[16,16,1024]{2,1,0:T(8,128)S(1)} async-done(((f32[16,16,1024]{2,1,0:T(8,128)}), f32[16,16,1024]{2,1,0:T(8,128)S(1)}, u32[]{:S(2)}, u32[]{:S(2)}) %all-to-all-start.4) | async-done | bytes 1048608 | tf_op jit(solution)/shard_map/all_to_all | solution.py:16
  222.7 0.1 reduce_sum.24
  222.8 0.9 fusion.4
  223.8 0.6 pad_maximum_fusion
  (13 shorter events, 0.2 us)
Async XLA Ops:
  0.0 106.5 %copy-start = (f32[8,128,128]{2,1,0:T(8,128)S(1)}, f32[8,128,128]{2,1,0:T(8,128)}, u32[]{:S(2)}) copy-start(f32[8,128,128]{2,1,0:T(8,128)} %param.7) | copy-start | bytes 1572868
  70.7 19.9 %copy-start.1 = (bf16[1,256,1024]{2,1,0:T(8,128)(2,1)S(1)}, bf16[1,256,1024]{2,1,0:T(8,128)(2,1)}, u32[]{:S(2)}) copy-start(bf16[1,256,1024]{2,1,0:T(8,128)(2,1)} %param.5) | copy-start | bytes 1572868
  83.2 23.1 %all-to-all-start.1 = ((f32[16,16,1024]{2,1,0:T(8,128)}), f32[16,16,1024]{2,1,0:T(8,128)S(1)}, u32[]{:S(2)}, u32[]{:S(2)}) async-start(f32[16,16,1024]{2,1,0:T(8,128)} %fusion.2), calls=%async_computation.1 | async-start | bytes 2097152 | tf_op jit(solution)/shard_map/all_to_all | solution.py:16
  90.5 21.8 %collective-permute-start = (bf16[1,256,1024]{2,1,0:T(8,128)(2,1)S(1)}, bf16[1,256,1024]{2,1,0:T(8,128)(2,1)}, u32[]{:S(2)}, u32[]{:S(2)}) collective-permute-start(bf16[1,256,1024]{2,1,0:T(8,128)(2,1)S(1)} %copy-done.1), channel_id=1, source_target_pairs={{0,8},{8,16},{16,24},{24,32},{32,40},{40,48},{48,56},{56,64},{64,7... | collective-permute-start | bytes 1572872 | tf_op jit(solution)/shard_map/ppermute | solution.py:38
  108.3 14.1 %all-to-all-start.2 = ((bf16[16,16,1024]{2,1,0:T(8,128)(2,1)}), bf16[16,16,1024]{2,1,0:T(8,128)(2,1)S(1)}, u32[]{:S(2)}, u32[]{:S(2)}) async-start(bf16[16,16,1024]{2,1,0:T(8,128)(2,1)} %broadcast_in_dim.2), calls=%async_computation.2 | async-start | bytes 1048576 | tf_op jit(solution)/shard_map/all_to_all | solution.py:28
  202.2 20.5 %all-to-all-start.4 = ((f32[16,16,1024]{2,1,0:T(8,128)}), f32[16,16,1024]{2,1,0:T(8,128)S(1)}, u32[]{:S(2)}, u32[]{:S(2)}) async-start(f32[16,16,1024]{2,1,0:T(8,128)} %fusion), calls=%async_computation.4 | async-start | bytes 2097152 | tf_op jit(solution)/shard_map/all_to_all | solution.py:16
